TPU v7x, 32 devices: a whole 2x2x4 slice. The times are simulated.
32 devices in a mesh: tiles: 16 (over z, y, x), grp: 2 (over core).
Axes of the slice: x: 2, y: 2, z: 4, core: 2. Of those that a mesh axis runs over, the one named last changes fastest.
Arguments:
- strips: bfloat16 [64, 256, 4096], P(('tiles', 'grp'))
- edge_colour: int32 [32, 2], P(('tiles', 'grp')), may hold values from 0 to 1, as said below
- patch_offsets: int32 [32, 2, 16, 2], P(('tiles', 'grp')), may hold values from 0 to 3968, as said below
- patch_live: int32 [32, 2], P(('tiles', 'grp')), may hold values from 4 to 16
- node_ids: int32 [32, 2, 16], P(('tiles', 'grp')), may hold values from 0 to 4095
Outputs:
- node_sums: float32 [2, 4096], P(None, ('tiles', 'grp'))
Inputs may be any that keep to these rules, and one draw needn't show every extreme that they name: `edge_colour`: for each device its 2 entries name different strips. `patch_offsets`: A device and the device it is paired with in a round have the same offsets in that round. Rows are at most 128.
All inputs are finite; a program needn't handle non-finite values.
Results may differ from a plain program's by a relative error of at most 0.0003.
Values may be sent and summed in bfloat16 or wider, within the bound.
A program may use at most 64 MiB of HBM per device.

v0:
```python
import math

import jax
import jax.numpy as jnp
from jax import lax
from jax.sharding import PartitionSpec as P

PATCH = 128
NODE_DEV = 128


highest = lax.Precision.HIGHEST


def from_partner(x, axis, stride):
    return lax.ppermute(x, axis, [(i, i ^ 1 << stride) for i in range(lax.axis_size(axis))])


def tables(length):
    indices = jnp.arange(length, dtype=jnp.int32)
    product = indices[:, None] * indices[None, :] % length
    angles = product.astype(jnp.float32) * (2.0 * math.pi / length)
    return (jnp.cos(angles), jnp.sin(angles))


def right_mul(patches, matrix):
    return jnp.einsum("pab,bc->pac", patches, matrix, precision=highest)


def left_mul(matrix, patches):
    return jnp.einsum("ab,pbc->pac", matrix, patches, precision=highest)


def forward(patches, cosine, sine):
    real_half = right_mul(patches, cosine)
    imag_half = -right_mul(patches, sine)
    return (
        left_mul(cosine, real_half) + left_mul(sine, imag_half),
        left_mul(cosine, imag_half) - left_mul(sine, real_half),
    )


def displacement_parts(first_set, second_set):
    length = first_set.shape[-1]
    cosine, sine = tables(length)
    first_real, first_imag = forward(first_set, cosine, sine)
    second_real, second_imag = forward(second_set, cosine, sine)
    cross_real = first_real * second_real + first_imag * second_imag
    cross_imag = first_imag * second_real - first_real * second_imag
    magnitude = jnp.sqrt(cross_real * cross_real + cross_imag * cross_imag)
    denominator = magnitude + 0.1 * jnp.mean(magnitude, axis=(1, 2), keepdims=True) + 1e-06
    white_real = cross_real / denominator
    white_imag = cross_imag / denominator
    back_real = left_mul(cosine, white_real) - left_mul(sine, white_imag)
    back_imag = left_mul(cosine, white_imag) + left_mul(sine, white_real)
    surface = (right_mul(back_real, cosine) - right_mul(back_imag, sine)) / float(length * length)
    flattened = surface.reshape(surface.shape[0], length * length)
    centre = jnp.mean(flattened, axis=1, keepdims=True)
    spread = jnp.sqrt(
        jnp.mean((flattened - centre) * (flattened - centre), axis=1, keepdims=True) + 1e-06
    )
    scores = 2.0 * (flattened - centre) / spread
    weights = jax.nn.softmax(scores, axis=-1).reshape(surface.shape)
    coords = ((jnp.arange(length, dtype=jnp.int32) + length // 2) % length - length // 2).astype(
        jnp.float32
    )
    coord_scale = float(length // 8)
    row_shift = jnp.sum(weights * coords[None, :, None], axis=(1, 2)) / coord_scale
    col_shift = jnp.sum(weights * coords[None, None, :], axis=(1, 2)) / coord_scale
    row_edge = jnp.sum(weights[:, length // 2, :], axis=1)
    col_edge = jnp.sum(weights[:, :, length // 2], axis=1)
    return (jnp.stack([row_shift, col_shift]), jnp.stack([row_edge, col_edge]))


def window_stack(strip, offsets, length):

    def single(corner):
        return lax.dynamic_slice(strip, (corner[0], corner[1]), (length, length))

    return jax.vmap(single)(offsets)


def on_device(strips, edge_colour, patch_offsets, patch_live, node_ids):
    rounds = strips.shape[0]
    length = PATCH
    slot_count = patch_offsets.shape[2]
    half_slots = slot_count // 2
    tile_count = lax.axis_size("tiles")
    group_count = lax.axis_size("grp")
    tile_index = lax.axis_index("tiles")
    kept_list = []
    partner_list = []
    side_list = []
    for round_index in range(rounds):
        pair_bit = 0 if round_index == 0 else tile_count.bit_length() - 2
        own_strip = lax.dynamic_index_in_dim(strips, edge_colour[0, round_index], 0, keepdims=False)
        own_windows = window_stack(own_strip, patch_offsets[0, round_index], length)
        pair_side = jnp.right_shift(tile_index, pair_bit) % 2
        kept_windows = lax.dynamic_slice_in_dim(own_windows, pair_side * half_slots, half_slots, 0)
        sent_windows = lax.dynamic_slice_in_dim(
            own_windows, (1 - pair_side) * half_slots, half_slots, 0
        )
        partner_windows = from_partner(sent_windows, "tiles", pair_bit)
        kept_list.append(kept_windows)
        partner_list.append(partner_windows)
        side_list.append(pair_side)
    first_set = jnp.concatenate(kept_list, axis=0).astype(jnp.float32)
    second_set = jnp.concatenate(partner_list, axis=0).astype(jnp.float32)
    computed, edge_mass = displacement_parts(first_set, second_set)
    mirrored = -computed - float(length) * edge_mass / float(length // 8)
    pieces = []
    for round_index in range(rounds):
        pair_bit = 0 if round_index == 0 else tile_count.bit_length() - 2
        own_part = computed[:, round_index * half_slots : (round_index + 1) * half_slots]
        sent_part = mirrored[:, round_index * half_slots : (round_index + 1) * half_slots]
        returned = from_partner(sent_part, "tiles", pair_bit)
        low_half = jnp.where(side_list[round_index] == 0, own_part, returned)
        high_half = jnp.where(side_list[round_index] == 0, returned, own_part)
        pieces.append(jnp.concatenate([low_half, high_half], axis=1))
    shifts = jnp.concatenate(pieces, axis=1)
    slot_index = jnp.arange(slot_count, dtype=jnp.int32)
    live_mask = (slot_index[None, :] < patch_live[0][:, None]).reshape(rounds * slot_count)
    values = jnp.where(live_mask[None, :], shifts, jnp.zeros_like(shifts))
    node_list = node_ids[0].reshape(rounds * slot_count)
    total_nodes = NODE_DEV * tile_count * group_count
    onehot = (node_list[:, None] == jnp.arange(total_nodes, dtype=jnp.int32)[None, :]).astype(
        jnp.float32
    )
    term_table = jnp.dot(values, onehot, precision=highest, preferred_element_type=jnp.float32)
    return lax.psum_scatter(term_table, ("tiles", "grp"), scatter_dimension=1, tiled=True)


def solution(mesh):
    placed = (
        P(("tiles", "grp"), None, None),
        P(("tiles", "grp"), None),
        P(("tiles", "grp"), None, None, None),
        P(("tiles", "grp"), None),
        P(("tiles", "grp"), None, None),
    )
    return jax.shard_map(
        on_device, mesh=mesh, in_specs=placed, out_specs=P(None, ("tiles", "grp")), check_vma=False
    )
```

profile of v0, /device:TPU:0, one launch (start us, length us, event | category | flops | bytes accessed | tf_op | source)
XLA Modules:
  0.0 288.2 jit_solution(8845961058801505626)
XLA Ops:
  6.5 1.4 fusion.155
  12.7 4.1 %dynamic-slice_bitcast_fusion.1 = (bf16[256,4096]{1,0:T(8,128)(2,1)S(1)}, bf16[256,4096]{1,0:T(8,128)(2,1)}) fusion(bf16[2,256,4096]{2,1,0:T(8,128)(2,1)} %param.5, s32[]{:T(128)S(6)} %select_n.130, s32[]{:T(128)S(6)} %select_n.134), kind=kLoop, calls=%fused_computation.6 | loop fusion | bytes 8388616 | tf_op jit(solution)/shard_map/jit(dynamic_index_in_dim)/squeeze | solution.py:96
  16.9 46.0 %while.3 = (s32[]{:T(128)}, bf16[256,4096]{1,0:T(8,128)(2,1)}, s32[16,2]{0,1:T(2,128)S(1)}, bf16[16,128,128]{2,1,0:T(8,128)(2,1)S(1)}, s32[]{:T(128)}) while((s32[]{:T(128)}, bf16[256,4096]{1,0:T(8,128)(2,1)}, s32[16,2]{0,1:T(2,128)S(1)}, bf16[16,128,128]{2,1,0:T(8,128)(2,1)S(1)}, s32[]{:T(128)}) %tuple.57), condition=%wide.while_cond.1, body=%wide.while_body.1.sunk | while | flops 2 | bytes 65645 | solution.py:78
  17.5 2.1 bitcast_dynamic-update-slice_fusion.5
  20.3 2.2 bitcast_dynamic-update-slice_fusion.5
  23.1 2.2 bitcast_dynamic-update-slice_fusion.5
  26.0 2.2 bitcast_dynamic-update-slice_fusion.5
  28.9 2.2 bitcast_dynamic-update-slice_fusion.5
  31.8 2.2 bitcast_dynamic-update-slice_fusion.5
  34.7 2.2 bitcast_dynamic-update-slice_fusion.5
  37.6 2.2 bitcast_dynamic-update-slice_fusion.5
  40.4 2.2 bitcast_dynamic-update-slice_fusion.5
  43.3 2.2 bitcast_dynamic-update-slice_fusion.5
  46.2 2.2 bitcast_dynamic-update-slice_fusion.5
  49.1 2.2 bitcast_dynamic-update-slice_fusion.5
  52.0 2.2 bitcast_dynamic-update-slice_fusion.5
  54.9 2.2 bitcast_dynamic-update-slice_fusion.5
  57.7 2.2 bitcast_dynamic-update-slice_fusion.5
  60.6 2.2 bitcast_dynamic-update-slice_fusion.5
  63.0 4.1 %collective-permute-start.1 = (bf16[8,128,128]{2,1,0:T(8,128)(2,1)S(1)}, bf16[8,128,128]{2,1,0:T(8,128)(2,1)}, u32[]{:S(2)}, u32[]{:S(2)}) collective-permute-start(bf16[8,128,128]{2,1,0:T(8,128)(2,1)S(1)} %get-tuple-element.51), channel_id=1, source_target_pairs={{0,16},{2,18},{4,20},{6,22},{8,24},{10,26},{12,28},{14,30},{16,0},... | collective-permute-start | bytes 786440 | tf_op jit(solution)/shard_map/ppermute | solution.py:16
  67.2 32.6 %while.2 = (s32[]{:T(128)}, bf16[256,4096]{1,0:T(8,128)(2,1)S(1)}, s32[16,2]{0,1:T(2,128)S(1)}, bf16[16,128,128]{2,1,0:T(8,128)(2,1)S(1)}, s32[]{:T(128)}) while((s32[]{:T(128)}, bf16[256,4096]{1,0:T(8,128)(2,1)S(1)}, s32[16,2]{0,1:T(2,128)S(1)}, bf16[16,128,128]{2,1,0:T(8,128)(2,1)S(1)}, s32[]{:T(128)}) %tuple.54), condition=%wide.while_cond, body=%wide.while_body.sunk | while | flops 2 | bytes 65645 | solution.py:78
  67.9 1.4 bitcast_dynamic-update-slice_fusion.4
  69.9 1.4 bitcast_dynamic-update-slice_fusion.4
  71.9 1.4 bitcast_dynamic-update-slice_fusion.4
  74.0 1.4 bitcast_dynamic-update-slice_fusion.4
  76.0 1.4 bitcast_dynamic-update-slice_fusion.4
  78.0 1.4 bitcast_dynamic-update-slice_fusion.4
  80.1 1.4 bitcast_dynamic-update-slice_fusion.4
  82.1 1.4 bitcast_dynamic-update-slice_fusion.4
  84.1 1.4 bitcast_dynamic-update-slice_fusion.4
  86.2 1.4 bitcast_dynamic-update-slice_fusion.4
  88.2 1.4 bitcast_dynamic-update-slice_fusion.4
  90.2 1.4 bitcast_dynamic-update-slice_fusion.4
  92.3 1.4 bitcast_dynamic-update-slice_fusion.4
  94.3 1.4 bitcast_dynamic-update-slice_fusion.4
  96.3 1.4 bitcast_dynamic-update-slice_fusion.4
  98.4 1.4 bitcast_dynamic-update-slice_fusion.4
  100.5 1.5 collective-permute-start
  102.0 0.8 convolution_negate_fusion.1
  102.8 0.8 fusion.8
  103.7 1.9 fusion.30
  105.6 1.2 fusion.36
  106.9 1.2 convolution_subtract_fusion.3
  108.6 1.0 constant_dynamic-update-slice_fusion.1
  109.6 1.0 constant_dynamic-update-slice_fusion
  110.6 0.8 fusion.34
  111.4 0.8 convolution_negate_fusion
  112.3 1.2 fusion.32
  113.5 1.9 fusion.28
  115.4 2.1 convolution_add_fusion.1
  117.6 1.2 convolution_subtract_fusion.2
  118.8 2.5 fusion.7
  121.3 1.8 fusion.22
  123.1 1.8 fusion.26
  124.9 1.8 fusion.1
  126.7 1.8 fusion.2
  128.6 1.4 fusion.24
  130.0 1.3 fusion.156
  133.7 1.5 collective-permute-start.2
  135.5 1.8 collective-permute-done.2
  137.3 2.4 collective-permute-done.3
  139.7 3.2 %convolution_bitcast_fusion = f32[4096,2]{1,0:T(8,128)} fusion(s32[32]{0:T(128)S(1)} %eq.32, f32[2,8]{1,0:T(2,128)S(1)} %get-tuple-element.61, f32[2,8]{1,0:T(2,128)S(1)} %get-tuple-element.62, f32[2,8]{1,0:T(2,128)S(1)} %get-tuple-element.56, f32[2,8]{1,0:T(2,128)S(1)} %get-tuple-element.55, pred[32]{0:T(512)(128)(4,1)S(1)} %lt.119), kind=kOutput, calls=%fused_computation.4 | convolution fusion | flops 3277056 | bytes 33184
  143.0 136.9 %reduce-scatter.4.cloned.1.call-done = f32[128,2]{1,0:T(8,128)} async-done(((f32[4096,2]{1,0:T(8,128)}), f32[128,2]{1,0:T(8,128)}) %reduce-scatter.4.cloned.1.call-update) | async-done | bytes 1040
  279.9 1.5 copy.29
  (99 shorter events, 25.4 us)
Async XLA Ops:
  6.5 273.4 %reduce-scatter.4.cloned.1.call-start = ((), (), s32[]{:S(2)}) async-start(), calls=%async_computation.1 | async-start | bytes 2162688
  63.0 46.6 %collective-permute-start.1 = (bf16[8,128,128]{2,1,0:T(8,128)(2,1)S(1)}, bf16[8,128,128]{2,1,0:T(8,128)(2,1)}, u32[]{:S(2)}, u32[]{:S(2)}) collective-permute-start(bf16[8,128,128]{2,1,0:T(8,128)(2,1)S(1)} %get-tuple-element.51), channel_id=1, source_target_pairs={{0,16},{2,18},{4,20},{6,22},{8,24},{10,26},{12,28},{14,30},{16,0},... | collective-permute-start | bytes 786440 | tf_op jit(solution)/shard_map/ppermute | solution.py:16
  100.5 8.1 %collective-permute-start = (bf16[8,128,128]{2,1,0:T(8,128)(2,1)}, bf16[8,128,128]{2,1,0:T(8,128)(2,1)}, u32[]{:S(2)}, u32[]{:S(2)}) collective-permute-start(bf16[8,128,128]{2,1,0:T(8,128)(2,1)} %get-tuple-element.53), channel_id=1, source_target_pairs={{0,2},{2,0},{4,6},{6,4},{8,10},{10,8},{12,14},{14,12},{16,18},{18,... | collective-permute-start | bytes 786440 | tf_op jit(solution)/shard_map/ppermute | solution.py:16
  106.9 1.3 copy-start.1
  106.9 1.4 copy-start
  133.7 3.6 %collective-permute-start.2 = (f32[2,8]{1,0:T(2,128)S(1)}, f32[2,8]{1,0:T(2,128)S(1)}, u32[]{:S(2)}, u32[]{:S(2)}) collective-permute-start(f32[2,8]{1,0:T(2,128)S(1)} %get-tuple-element.63), channel_id=1, source_target_pairs={{0,2},{2,0},{4,6},{6,4},{8,10},{10,8},{12,14},{14,12},{16,18},{18,... | collective-permute-start | bytes 200 | tf_op jit(solution)/shard_map/ppermute | solution.py:16
  135.2 4.5 %collective-permute-start.3 = (f32[2,8]{1,0:T(2,128)S(1)}, f32[2,8]{1,0:T(2,128)S(1)}, u32[]{:S(2)}, u32[]{:S(2)}) collective-permute-start(f32[2,8]{1,0:T(2,128)S(1)} %get-tuple-element.64), channel_id=1, source_target_pairs={{0,16},{2,18},{4,20},{6,22},{8,24},{10,26},{12,28},{14,30},{16,0},... | collective-permute-start | bytes 200 | tf_op jit(solution)/shard_map/ppermute | solution.py:16
Sparse Core Ops, SparseCore 0:
  143.1 136.7 reduce-scatter.3
where the time goes:
time: 290 us; the launch traced here: 288 us
  waiting for transfers between devices  141 us (49%)
  local copies, waits for them, and re-layouts  88.9 us (31%)
  matrix products  30 us (10%)
  between operations  17.7 us (6%)
  starting transfers between devices  7.44 us (3%)
    unnamed x2, waiting for transfers between devices  137 us
    gather x96, local copies, waits for them, and re-layouts  78.1 us
    dot_general x12, matrix products, left_mul(): return jnp.einsum('ab,pbc->pac', matrix, patches, precision=highest)  20.6 us
    ppermute x4, starting transfers between devices, from_partner(): lax.ppermute(x, axis, [(i, i ^ 1 << stride) for i in range(lax.axis_size(...  7.44 us
    dot_general x6, matrix products, right_mul(): return jnp.einsum('pab,bc->pac', patches, matrix, precision=highest)  6.11 us
  transfers between devices with their start and end apart: 5, of which 4 were waited for; matrix products, arithmetic and copies ran while one was open for 14% of the time, Pallas kernels for 0%

commit v1 on v0

v1 whole, which is shorter than its diff:
```python
import functools
import math

import jax
import jax.numpy as jnp
import numpy as np
from jax import lax
from jax.experimental import pallas as pl
from jax.experimental.pallas import tpu as pltpu
from jax.sharding import PartitionSpec as P

PATCH = 128
NODE_DEV = 128
LANES = 128
PACK = 4

F32 = jnp.float32
BF16 = jnp.bfloat16
VMEM = pltpu.MemorySpace.VMEM
SMEM = pltpu.MemorySpace.SMEM


def split_np(x):
    hi = np.asarray(x, np.float32).astype(BF16)
    lo = (np.asarray(x, np.float64) - hi.astype(np.float64)).astype(np.float32).astype(BF16)
    return hi, lo


def tables():
    n = PATCH
    j = np.arange(n)
    angle = 2.0 * math.pi / n * ((j[:, None] * j[None, :]) % n)
    c, s = np.cos(angle), np.sin(angle)
    chi, clo = split_np(np.concatenate([c, s], axis=1))
    col = np.concatenate([chi, clo], axis=0)
    rhi, rlo = split_np(np.block([[c, -s], [s, c]]))
    row = np.concatenate([rhi, rlo, rhi], axis=1)
    ihi, ilo = split_np(np.concatenate([c, s], axis=1))
    inv_row = np.concatenate([ihi, ilo, ihi], axis=1)
    weight = np.where((j == 0) | (j == n // 2), 1.0, 2.0)[:, None]
    packed = np.where(j[:, None] <= n // 2, weight * c, -2.0 * s) / float(n * n)
    vhi, vlo = split_np(packed)
    inv_col = np.concatenate([vhi, vlo, vhi], axis=0)
    return col, row, inv_row, inv_col


def split(x):
    hi = x.astype(BF16)
    return hi, (x - hi.astype(F32)).astype(BF16)


def dot(a, b):
    return jnp.dot(a, b, preferred_element_type=F32)


def extract(half, colour_ref, offset_ref, strip_ref, kept_ref, sent_ref, tmp_ref):
    n = PATCH
    slots = 2 * half
    rnd = pl.program_id(0)
    tile = lax.axis_index("tiles")
    top = lax.axis_size("tiles").bit_length() - 2
    side = jnp.where(rnd == 0, tile % 2, (tile // (1 << top)) % 2)
    height, width = strip_ref.shape[1], strip_ref.shape[2]

    def place(j):
        k = (side * half + j) % slots
        return offset_ref[0, rnd, k, 0], offset_ref[0, rnd, k, 1]

    for j in range(slots):
        row, column = place(j)
        left = jnp.minimum(column // LANES, width // LANES - 2) * LANES
        upper = jnp.minimum(row // 16, (height - n) // 16 - 1) * 16
        block = strip_ref[
            0, pl.ds(pl.multiple_of(upper, 16), n + 16), pl.ds(pl.multiple_of(left, LANES), 2 * LANES)
        ].astype(F32)
        shift = (2 * LANES - (column - left)) % (2 * LANES)
        tmp_ref[j] = pltpu.roll(block, shift, 1)[:, :n]
    for j in range(slots):
        row, column = place(j)
        upper = jnp.minimum(row // 16, (height - n) // 16 - 1) * 16
        window = tmp_ref[j, pl.ds(row - upper, n), :].astype(BF16)
        if j < half:
            kept_ref[0, j] = window
        else:
            sent_ref[0, j - half] = window


def row_place(column, base):
    count = column.shape[0]
    lane = lax.broadcasted_iota(jnp.int32, (count, LANES), 1)
    sub = lax.broadcasted_iota(jnp.int32, (count, LANES), 0)
    return jnp.sum(jnp.where(lane == sub + base, column, 0.0), axis=0, keepdims=True)


def correlate(first, second, col, row, inv_row, inv_col):
    n = PATCH
    count = first.shape[0]
    lane = lax.broadcasted_iota(jnp.int32, (n, n), 1)
    low = lane <= n // 2
    crosses = []
    mag_sums = []
    for p in range(count):
        x = jnp.concatenate([first[p], second[p]], axis=0)
        y = dot(jnp.concatenate([x, x], axis=1), col)
        hi, lo = split(y)

        def stack(v):
            return jnp.concatenate(
                [
                    jnp.concatenate([v[:n, :n], v[n:, :n]], axis=1),
                    jnp.concatenate([v[:n, n:], v[n:, n:]], axis=1),
                ],
                axis=0,
            )

        hi, lo = stack(hi), stack(lo)
        f = dot(row, jnp.concatenate([hi, hi, lo], axis=0))
        r1, r2 = f[:n, :n], f[:n, n:]
        i1, i2 = f[n:, :n], f[n:, n:]
        cross_r = r1 * r2 + i1 * i2
        cross_i = r1 * i2 - i1 * r2
        mag = jnp.sqrt(cross_r * cross_r + cross_i * cross_i)
        crosses.append((cross_r, cross_i, mag))
        mag_sums.append(jnp.sum(mag, axis=0, keepdims=True))
    mean = jnp.sum(jnp.concatenate(mag_sums, axis=0), axis=1, keepdims=True) / float(n * n)
    extra = 0.1 * mean + 1e-06
    surfaces = []
    sums = []
    for p in range(count):
        cross_r, cross_i, mag = crosses[p]
        inverse = 1.0 / (mag + extra[p : p + 1])
        g_r = cross_r * inverse
        g_i = cross_i * inverse
        g = jnp.concatenate([jnp.where(low, g_r, g_i), jnp.where(low, -g_i, g_r)], axis=0)
        hi, lo = split(g)
        b = dot(inv_row, jnp.concatenate([hi, hi, lo], axis=0))
        bhi, blo = split(b)
        surface = dot(jnp.concatenate([bhi, bhi, blo], axis=1), inv_col)
        surfaces.append(surface)
        sums.append(jnp.sum(surface, axis=0, keepdims=True))
    centre = jnp.sum(jnp.concatenate(sums, axis=0), axis=1, keepdims=True) / float(n * n)
    squares = []
    tops = []
    for p in range(count):
        deviation = surfaces[p] - centre[p : p + 1]
        squares.append(jnp.sum(deviation * deviation, axis=0, keepdims=True))
        tops.append(jnp.max(surfaces[p], axis=0, keepdims=True))
    variance = jnp.sum(jnp.concatenate(squares, axis=0), axis=1, keepdims=True) / float(n * n)
    top = jnp.max(jnp.concatenate(tops, axis=0), axis=1, keepdims=True)
    scale = 2.0 / jnp.sqrt(variance + 1e-06)
    sub = lax.broadcasted_iota(jnp.int32, (n, n), 0)
    sub_coord = ((sub + n // 2) % n - n // 2).astype(F32)
    columns = []
    rows = []
    edges = []
    for p in range(count):
        e = jnp.exp((surfaces[p] - top[p : p + 1]) * scale[p : p + 1])
        columns.append(jnp.sum(e, axis=0, keepdims=True))
        rows.append(jnp.sum(e * sub_coord, axis=0, keepdims=True))
        edges.append(e[n // 2 : n // 2 + 1, :])
    columns = jnp.concatenate(columns, axis=0)
    rows = jnp.concatenate(rows, axis=0)
    edges = jnp.concatenate(edges, axis=0)
    lane = lax.broadcasted_iota(jnp.int32, (count, n), 1)
    lane_coord = ((lane + n // 2) % n - n // 2).astype(F32)

    def total(v):
        return jnp.sum(v, axis=1, keepdims=True)

    unit = float(n // 8)
    norm = 1.0 / total(columns)
    row_shift = total(rows) * norm / unit
    col_shift = total(columns * lane_coord) * norm / unit
    row_edge = total(edges) * norm * (float(n) / unit)
    col_edge = total(jnp.where(lane == n // 2, columns, 0.0)) * norm * (float(n) / unit)
    return row_shift, col_shift, -row_shift - row_edge, -col_shift - col_edge


def terms(base, last, first_ref, second_ref, col_ref, row_ref, inv_row_ref, inv_col_ref, *rest):
    count = first_ref.shape[1]
    a, b, c, d = correlate(
        first_ref[0], second_ref[0], col_ref[...], row_ref[...], inv_row_ref[...], inv_col_ref[...]
    )
    row_line = row_place(a, base) + row_place(c, base + count)
    col_line = row_place(b, base) + row_place(d, base + count)
    if last:
        ids_ref, before_ref, out_ref = rest
        row_line = row_line + before_ref[0:1, :]
        col_line = col_line + before_ref[1:2, :]
        id_line = ids_ref[...]
    else:
        (out_ref,) = rest
        id_line = jnp.zeros_like(row_line)
    tile = jnp.concatenate([row_line, col_line, id_line, jnp.zeros((5, LANES), F32)], axis=0)
    if last:
        me = lax.axis_index("tiles") * lax.axis_size("grp") + lax.axis_index("grp")
        tile = pltpu.roll(tile, (me % PACK) * (LANES // PACK), 1)
    out_ref[...] = tile


def gather(devices, tile_ref, out_ref, buf, send_sem, recv_sem):
    groups = lax.axis_size("grp")
    me = lax.axis_index("tiles") * groups + lax.axis_index("grp")
    barrier = pltpu.get_barrier_semaphore()

    def where(i):
        d = lax.rem(me + i, devices)
        return d, (d // groups, d % groups)

    def greet(i, _):
        d, at = where(i)
        pl.semaphore_signal(barrier, inc=1, device_id=at, device_id_type=pl.DeviceIdType.MESH)
        return 0

    lax.fori_loop(1, devices, greet, 0)
    pl.semaphore_wait(barrier, devices - 1)

    def copy(i):
        d, at = where(i)
        return pltpu.make_async_remote_copy(
            src_ref=tile_ref,
            dst_ref=buf.at[i],
            send_sem=send_sem.at[i],
            recv_sem=recv_sem.at[i],
            device_id=at,
            device_id_type=pl.DeviceIdType.MESH,
        )

    def start(i, _):
        copy(i).start()
        return 0

    def finish(i, _):
        copy(i).wait()
        return 0

    lax.fori_loop(1, devices, start, 0)
    buf[0] = tile_ref[...]
    lax.fori_loop(1, devices, finish, 0)
    node = lax.broadcasted_iota(jnp.int32, (NODE_DEV, LANES), 0).astype(F32)
    first_node = (me * NODE_DEV).astype(F32)
    acc = jnp.zeros((8, NODE_DEV), F32)
    for g in range(devices // PACK):
        tile = buf[g * PACK]
        for i in range(1, PACK):
            tile = tile + buf[g * PACK + i]
        onehot = jnp.where(tile[2:3, :] - first_node == node, 1.0, 0.0).astype(BF16)
        hi = tile.astype(BF16)
        rest = tile - hi.astype(F32)
        mid = rest.astype(BF16)
        low = (rest - mid.astype(F32)).astype(BF16)
        stacked = jnp.concatenate([hi, mid, low, jnp.zeros_like(hi)], axis=0)
        part = lax.dot_general(
            stacked, onehot, (((1,), (1,)), ((), ())), preferred_element_type=F32
        )
        acc = acc + (part[0:8] + part[8:16] + part[16:24])
    out_ref[...] = acc[0:2]


def on_device(strips, edge_colour, patch_offsets, patch_live, node_ids):
    rounds = strips.shape[0]
    height, width = strips.shape[1:]
    n = PATCH
    slot_count = patch_offsets.shape[2]
    half = slot_count // 2
    tile_count = lax.axis_size("tiles")
    devices = tile_count * lax.axis_size("grp")
    tile_index = lax.axis_index("tiles")
    col, row, inv_row, inv_col = (jnp.asarray(t) for t in tables())
    window_spec = pl.BlockSpec((1, half, n, n), lambda r, *_: (r, 0, 0, 0))
    kept, sent = pl.pallas_call(
        functools.partial(extract, half),
        out_shape=[jax.ShapeDtypeStruct((rounds, half, n, n), BF16)] * 2,
        grid_spec=pltpu.PrefetchScalarGridSpec(
            num_scalar_prefetch=2,
            grid=(rounds,),
            in_specs=[pl.BlockSpec((1, height, width), lambda r, colour, _: (colour[0, r], 0, 0))],
            out_specs=[window_spec, window_spec],
            scratch_shapes=[pltpu.VMEM((slot_count, n + 16, n), F32)],
        ),
        name="extract",
    )(edge_colour, patch_offsets, strips)

    slot = jnp.arange(slot_count, dtype=jnp.int32)
    ids = jnp.where(slot[None, :] < patch_live[0][:, None], node_ids[0], -1)
    seconds = []
    lines = []
    for r in range(rounds):
        bit = 0 if r == 0 else tile_count.bit_length() - 2
        pairs = [(i, i ^ (1 << bit)) for i in range(tile_count)]
        side = jnp.right_shift(tile_index, bit) % 2
        seconds.append(lax.ppermute(sent[r : r + 1], "tiles", pairs))
        mine = jnp.where(side == 0, ids[r, :half], ids[r, half:])
        other = jnp.where(side == 0, ids[r, half:], ids[r, :half])
        lines += [mine, lax.ppermute(other, "tiles", pairs)]
    id_line = jnp.concatenate(lines).astype(F32)
    id_line = jnp.concatenate([id_line, jnp.full((LANES - id_line.shape[0],), 0.0, F32)])[None, :]

    whole = pl.BlockSpec(memory_space=VMEM)
    tile = None
    for r in range(rounds):
        last = r == rounds - 1
        args = [kept[r : r + 1], seconds[r], col, row, inv_row, inv_col]
        if last:
            args += [id_line, tile]
        tile = pl.pallas_call(
            functools.partial(terms, r * slot_count, last),
            out_shape=jax.ShapeDtypeStruct((8, LANES), F32),
            in_specs=[whole] * len(args),
            out_specs=whole,
            name="terms%d" % r,
            cost_estimate=pl.CostEstimate(
                flops=2 * half * n * n * n * 40, bytes_accessed=4 * half * n * n, transcendentals=half * n * n
            ),
        )(*args)

    return pl.pallas_call(
        functools.partial(gather, devices),
        out_shape=jax.ShapeDtypeStruct((2, NODE_DEV), F32),
        in_specs=[whole],
        out_specs=whole,
        scratch_shapes=[
            pltpu.VMEM((devices, 8, LANES), F32),
            pltpu.SemaphoreType.DMA((devices,)),
            pltpu.SemaphoreType.DMA((devices,)),
        ],
        compiler_params=pltpu.CompilerParams(collective_id=0, has_side_effects=True),
        name="gather",
    )(tile)


def solution(mesh):
    placed = (
        P(("tiles", "grp"), None, None),
        P(("tiles", "grp"), None),
        P(("tiles", "grp"), None, None, None),
        P(("tiles", "grp"), None),
        P(("tiles", "grp"), None, None),
    )
    return jax.shard_map(
        on_device, mesh=mesh, in_specs=placed, out_specs=P(None, ("tiles", "grp")), check_vma=False
    )
```

time: 290 us -> 49.6 us (0.17)
  waiting for transfers between devices: 141 us -> 7.9 us
  local copies, waits for them, and re-layouts: 88.9 us -> 7.5 us
  matrix products: 30 us -> 0 us
  Pallas kernels: 0 us -> 27.4 us
  between operations: 17.7 us -> 0.03 us
    unnamed x2 -> x0, waiting for transfers between devices: 137 us -> none
    gather x96 -> x0, local copies, waits for them, and re-layouts: 78.1 us -> none
    pallas_call x0 -> x4, Pallas kernels: none -> 27.4 us  [the longest x2 12.2 us: on_device(): pl.pallas_call(functools.partial(terms, r * slot_count, last), out_shape=...]
    dot_general x18 -> x0, matrix products: 26.7 us -> none  [the longest x12 20.6 us: left_mul(): return jnp.einsum('ab,pbc->pac', matrix, patches, precision=highest)]
    squeeze x2 -> x0, local copies, waits for them, and re-layouts: 4.78 us -> none  [the longest x1 4.08 us: on_device(): lax.dynamic_index_in_dim(strips, edge_colour[0, round_index], 0, keepdims...]
    ppermute x4, waiting for transfers between devices: 4.36 us -> 7.9 us  [the longest x2 7.9 us: on_device(): lines += [mine, lax.ppermute(other, 'tiles', pairs)]]
    unnamed x1 -> x0, matrix products: 3.24 us -> none
  transfers between devices with their start and end apart: 5 -> 4, of which waited for: 4 -> 1; matrix products, arithmetic and copies ran while one was open for 14% -> 5% of each run, Pallas kernels for 0% -> 12%
where the time goes in v1:
time: 49.6 us; the launch traced here: 49.2 us
  Pallas kernels  27.4 us (55%)
  waiting for transfers between devices  7.9 us (16%)
  local copies, waits for them, and re-layouts  7.5 us (15%)
  starting transfers between devices  6.24 us (13%)
    pallas_call x2, Pallas kernels, on_device(): pl.pallas_call(functools.partial(terms, r * slot_count, last), out_shape=...  12.2 us
    pallas_call x1, Pallas kernels, on_device(): pl.pallas_call(functools.partial(gather, devices), out_shape=jax.ShapeDty...  10.6 us
    ppermute x2, waiting for transfers between devices, on_device(): lines += [mine, lax.ppermute(other, 'tiles', pairs)]  7.9 us
    pallas_call x1, Pallas kernels, on_device(): pl.pallas_call(functools.partial(extract, half), out_shape=[jax.ShapeDtyp...  4.53 us
    ppermute x2, starting transfers between devices, on_device(): seconds.append(lax.ppermute(sent[r:r + 1], 'tiles', pairs))  4.41 us
    unnamed x10, local copies, waits for them, and re-layouts  4.04 us
    slice x1, local copies, waits for them, and re-layouts, on_device(): args = [kept[r:r + 1], seconds[r], col, row, inv_row, inv_col]  1.87 us
    ppermute x2, starting transfers between devices, on_device(): lines += [mine, lax.ppermute(other, 'tiles', pairs)]  1.83 us
  transfers between devices with their start and end apart: 4, of which 1 were waited for; matrix products, arithmetic and copies ran while one was open for 5% of the time, Pallas kernels for 12%

profile of v1, /device:TPU:0, one launch (start us, length us, event | category | flops | bytes accessed | tf_op | source)
XLA Modules:
  0.0 49.2 jit_solution(17882249512254247629)
XLA Ops:
  0.0 0.0 copy-start
  0.0 0.0 copy-start.1
  0.0 1.4 %copy.10.offset_ref = s32[1,2,16,2]{3,2,1,0:T(8,128)} copy(s32[1,2,16,2]{2,3,1,0:T(2,128)} %param.11) | data formatting | bytes 512 | tf_op args[2]
  1.4 4.5 %extract.1 = (bf16[2,8,128,128]{3,2,1,0:T(8,128)(2,1)}, bf16[2,8,128,128]{3,2,1,0:T(8,128)(2,1)}) custom-call(s32[1,2]{1,0:T(1,128)} %colour_ref.1, s32[1,2,16,2]{3,2,1,0:T(8,128)} %copy.10.offset_ref, bf16[2,256,4096]{2,1,0:T(8,128)(2,1)} %strip_ref.1), custom_call_target="tpu_custom_call" | custom-call | tf_op jit(solution)/shard_map/extract/pallas_call | solution.py:271
  5.9 1.1 %fusion.4 = (bf16[1,8,128,128]{3,2,1,0:T(8,128)(2,1)S(1)}, bf16[1,8,128,128]{3,2,1,0:T(8,128)(2,1)S(1)}) fusion(bf16[2,8,128,128]{3,2,1,0:T(8,128)(2,1)} %get-tuple-element.8), kind=kLoop, calls=%fused_computation.11 | loop fusion | bytes 1048576 | tf_op jit(solution)/shard_map/slice | solution.py:292
  7.0 4.1 %collective-permute-start = (bf16[1,8,128,128]{3,2,1,0:T(8,128)(2,1)S(1)}, bf16[1,8,128,128]{3,2,1,0:T(8,128)(2,1)S(1)}, u32[]{:S(2)}, u32[]{:S(2)}) collective-permute-start(bf16[1,8,128,128]{3,2,1,0:T(8,128)(2,1)S(1)} %get-tuple-element.10), channel_id=1, source_target_pairs={{0,16},{2,18},{4,20},{6,22},{8,24},{10,26},{12,28},{14,30},{16,0},... | collective-permute-start | bytes 786440 | tf_op jit(solution)/shard_map/ppermute | solution.py:292
  11.1 0.0 copy-done
  11.1 0.0 copy-done.1
  11.1 0.1 compare_select_fusion
  11.2 0.1 fusion
  11.3 0.1 collective-permute-start.2
  11.3 1.8 %collective-permute-start.1 = (s32[8]{0:T(128)S(1)}, s32[8]{0:T(128)S(1)}, u32[]{:S(2)}, u32[]{:S(2)}) collective-permute-start(s32[8]{0:T(128)S(1)} %get-tuple-element.16), channel_id=1, source_target_pairs={{0,2},{2,0},{4,6},{6,4},{8,10},{10,8},{12,14},{14,12},{16,18},{18,... | collective-permute-start | bytes 104 | tf_op jit(solution)/shard_map/ppermute | solution.py:295
  13.1 0.3 collective-permute-start.3
  13.4 1.9 %fusion.5 = (bf16[1,8,128,128]{3,2,1,0:T(8,128)(2,1)}, bf16[1,8,128,128]{3,2,1,0:T(8,128)(2,1)}) fusion(bf16[2,8,128,128]{3,2,1,0:T(8,128)(2,1)} %get-tuple-element.7), kind=kLoop, calls=%fused_computation.12 | loop fusion | bytes 1048576 | tf_op jit(solution)/shard_map/slice | solution.py:303
  15.3 7.9 %collective-permute-done.2 = s32[8]{0:T(128)S(1)} collective-permute-done((s32[8]{0:T(128)S(1)}, s32[8]{0:T(128)S(1)}, u32[]{:S(2)}, u32[]{:S(2)}) %collective-permute-start.2) | collective-permute-done | bytes 64 | tf_op jit(solution)/shard_map/ppermute | solution.py:295
  23.2 0.0 collective-permute-done.1
  23.2 0.1 add_convert_fusion
  23.2 0.5 %pad_bitcast_fusion.rest_0_ = f32[1,128]{1,0:T(1,128)} fusion(f32[32]{0:T(128)S(1)} %add_convert_fusion), kind=kLoop, calls=%fused_computation.10 | loop fusion | bytes 640 | tf_op jit(solution)/shard_map/broadcast_in_dim | solution.py:297
  23.8 0.0 collective-permute-done.3.second_ref
  23.8 0.0 copy-start.3
  23.8 0.7 %copy-done.3 = bf16[1,8,128,128]{3,2,1,0:T(8,128)(2,1)} copy-done((bf16[1,8,128,128]{3,2,1,0:T(8,128)(2,1)}, bf16[1,8,128,128]{3,2,1,0:T(8,128)(2,1)S(1)}, u32[]{:S(2)}) %copy-start.3) | copy-done | bytes 262168
  24.5 6.1 %terms0.1.rest_1_ = f32[8,128]{1,0:T(8,128)} custom-call(bf16[1,8,128,128]{3,2,1,0:T(8,128)(2,1)} %get-tuple-element.11.first_ref, bf16[1,8,128,128]{3,2,1,0:T(8,128)(2,1)} %copy-done.3, bf16[256,256]{1,0:T(8,128)(2,1)} %constant.38.clone.col_ref, bf16[256,768]{1,0:T(8,128)(2,1)} %constant.39.clone.row_ref, bf16[128,768]{1,0:T(8,128)(2,1)} %constant.40.clone.inv_row_ref, ...), custom_call_target="tpu_custom_call" | custom-call | flops 1342177280 | bytes 524288 | tf_op jit(solution)/shard_map/terms0/pallas_call | solution.py:306
  30.5 0.0 collective-permute-done.second_ref
  30.6 0.0 copy-start.2
  30.6 0.7 %copy-done.2 = bf16[1,8,128,128]{3,2,1,0:T(8,128)(2,1)} copy-done((bf16[1,8,128,128]{3,2,1,0:T(8,128)(2,1)}, bf16[1,8,128,128]{3,2,1,0:T(8,128)(2,1)S(1)}, u32[]{:S(2)}) %copy-start.2) | copy-done | bytes 262168
  31.3 6.1 %terms1.1.tile_ref = f32[8,128]{1,0:T(8,128)} custom-call(bf16[1,8,128,128]{3,2,1,0:T(8,128)(2,1)} %get-tuple-element.12.first_ref, bf16[1,8,128,128]{3,2,1,0:T(8,128)(2,1)} %copy-done.2, bf16[256,256]{1,0:T(8,128)(2,1)} %constant.38.clone.col_ref, bf16[256,768]{1,0:T(8,128)(2,1)} %constant.39.clone.row_ref, bf16[128,768]{1,0:T(8,128)(2,1)} %constant.40.clone.inv_row_ref, ...), custom_call_target="tpu_custom_call" | custom-call | flops 1342177280 | bytes 524288 | tf_op jit(solution)/shard_map/terms1/pallas_call | solution.py:306
  37.4 10.6 %gather.1 = f32[2,128]{1,0:T(2,128)} custom-call(f32[8,128]{1,0:T(8,128)} %terms1.1.tile_ref), custom_call_target="tpu_custom_call" | custom-call | tf_op jit(solution)/shard_map/gather/pallas_call | solution.py:317
  48.0 1.2 %copy.12 = f32[2,128]{1,0:T(2,128)} copy(f32[2,128]{1,0:T(2,128)} %gather.1) | data formatting | bytes 2048
Async XLA Ops:
  0.0 11.1 %copy-start = (s32[1,2,16]{2,1,0:T(2,128)S(1)}, s32[1,2,16]{2,1,0:T(2,128)}, u32[]{:S(2)}) copy-start(s32[1,2,16]{2,1,0:T(2,128)} %param.13) | copy-start | bytes 388
  0.0 11.1 %copy-start.1 = (s32[1,2]{1,0:T(1,128)S(1)}, s32[1,2]{1,0:T(1,128)}, u32[]{:S(2)}) copy-start(s32[1,2]{1,0:T(1,128)} %param.12) | copy-start | bytes 28
  7.0 23.6 %collective-permute-start = (bf16[1,8,128,128]{3,2,1,0:T(8,128)(2,1)S(1)}, bf16[1,8,128,128]{3,2,1,0:T(8,128)(2,1)S(1)}, u32[]{:S(2)}, u32[]{:S(2)}) collective-permute-start(bf16[1,8,128,128]{3,2,1,0:T(8,128)(2,1)S(1)} %get-tuple-element.10), channel_id=1, source_target_pairs={{0,16},{2,18},{4,20},{6,22},{8,24},{10,26},{12,28},{14,30},{16,0},... | collective-permute-start | bytes 786440 | tf_op jit(solution)/shard_map/ppermute | solution.py:292
  11.3 11.9 %collective-permute-start.2 = (s32[8]{0:T(128)S(1)}, s32[8]{0:T(128)S(1)}, u32[]{:S(2)}, u32[]{:S(2)}) collective-permute-start(s32[8]{0:T(128)S(1)} %get-tuple-element.15), channel_id=1, source_target_pairs={{0,16},{2,18},{4,20},{6,22},{8,24},{10,26},{12,28},{14,30},{16,0},... | collective-permute-start | bytes 104 | tf_op jit(solution)/shard_map/ppermute | solution.py:295
  11.3 11.8 %collective-permute-start.1 = (s32[8]{0:T(128)S(1)}, s32[8]{0:T(128)S(1)}, u32[]{:S(2)}, u32[]{:S(2)}) collective-permute-start(s32[8]{0:T(128)S(1)} %get-tuple-element.16), channel_id=1, source_target_pairs={{0,2},{2,0},{4,6},{6,4},{8,10},{10,8},{12,14},{14,12},{16,18},{18,... | collective-permute-start | bytes 104 | tf_op jit(solution)/shard_map/ppermute | solution.py:295
  13.1 10.7 %collective-permute-start.3 = (bf16[1,8,128,128]{3,2,1,0:T(8,128)(2,1)S(1)}, bf16[1,8,128,128]{3,2,1,0:T(8,128)(2,1)S(1)}, u32[]{:S(2)}, u32[]{:S(2)}) collective-permute-start(bf16[1,8,128,128]{3,2,1,0:T(8,128)(2,1)S(1)} %get-tuple-element.9), channel_id=1, source_target_pairs={{0,2},{2,0},{4,6},{6,4},{8,10},{10,8},{12,14},{14,12},{16,18},{18,... | collective-permute-start | bytes 786440 | tf_op jit(solution)/shard_map/ppermute | solution.py:292
  23.8 0.7 %copy-start.3 = (bf16[1,8,128,128]{3,2,1,0:T(8,128)(2,1)}, bf16[1,8,128,128]{3,2,1,0:T(8,128)(2,1)S(1)}, u32[]{:S(2)}) copy-start(bf16[1,8,128,128]{3,2,1,0:T(8,128)(2,1)S(1)} %collective-permute-done.3.second_ref) | copy-start | bytes 786436
  30.6 0.7 %copy-start.2 = (bf16[1,8,128,128]{3,2,1,0:T(8,128)(2,1)}, bf16[1,8,128,128]{3,2,1,0:T(8,128)(2,1)S(1)}, u32[]{:S(2)}) copy-start(bf16[1,8,128,128]{3,2,1,0:T(8,128)(2,1)S(1)} %collective-permute-done.second_ref) | copy-start | bytes 786436

commit v2 on v1

v2 whole, which is shorter than its diff:
```python
import functools
import math

import jax
import jax.numpy as jnp
import numpy as np
from jax import lax
from jax.experimental import pallas as pl
from jax.experimental.pallas import tpu as pltpu
from jax.sharding import PartitionSpec as P

PATCH = 128
NODE_DEV = 128
LANES = 128
PACK = 4
GROUP = 4

F32 = jnp.float32
BF16 = jnp.bfloat16
VMEM = pltpu.MemorySpace.VMEM
SMEM = pltpu.MemorySpace.SMEM


def split_np(x):
    hi = np.asarray(x, np.float32).astype(BF16)
    lo = (np.asarray(x, np.float64) - hi.astype(np.float64)).astype(np.float32).astype(BF16)
    return hi, lo


def tables():
    n = PATCH
    j = np.arange(n)
    angle = 2.0 * math.pi / n * ((j[:, None] * j[None, :]) % n)
    c, s = np.cos(angle), np.sin(angle)
    chi, clo = split_np(np.concatenate([c, s], axis=1))
    col = np.concatenate([chi, clo], axis=0)
    rhi, rlo = split_np(np.block([[c, -s], [s, c]]))
    row = np.concatenate([rhi, rlo, rhi], axis=1)
    ihi, ilo = split_np(np.concatenate([c, s], axis=1))
    inv_row = np.concatenate([ihi, ilo, ihi], axis=1)
    weight = np.where((j == 0) | (j == n // 2), 1.0, 2.0)[:, None]
    packed = np.where(j[:, None] <= n // 2, weight * c, -2.0 * s) / float(n * n)
    vhi, vlo = split_np(packed)
    inv_col = np.concatenate([vhi, vlo, vhi], axis=0)
    return col, row, inv_row, inv_col


def split(x):
    hi = x.astype(BF16)
    return hi, (x - hi.astype(F32)).astype(BF16)


def dot(a, b):
    return jnp.dot(a, b, preferred_element_type=F32)


def extract(half, colour_ref, offset_ref, live_ref, ids_ref, strip_ref, kept_ref, sent_ref, line_ref, tmp_ref):
    n = PATCH
    slots = 2 * half
    rnd = pl.program_id(0)
    tile = lax.axis_index("tiles")
    side = jnp.where(rnd == 0, tile % 2, (tile // (lax.axis_size("tiles") // 2)) % 2)
    height, width = strip_ref.shape[1], strip_ref.shape[2]
    rows = []
    for j in range(slots):
        k = (side * half + half + j) % slots
        row, column = offset_ref[0, rnd, 0, k], offset_ref[0, rnd, 1, k]
        left = jnp.minimum(lax.div(column, LANES), width // LANES - 2) * LANES
        upper = jnp.minimum(lax.div(row, 16), (height - n) // 16 - 1) * 16
        block = strip_ref[
            0, pl.ds(pl.multiple_of(upper, 16), n + 16), pl.ds(pl.multiple_of(left, LANES), 2 * LANES)
        ].astype(F32)
        shift = lax.rem(2 * LANES - (column - left), 2 * LANES)
        tmp_ref[j] = pltpu.roll(block, shift, 1)[:, :n]
        rows.append(row - upper)
    for j in range(slots):
        window = tmp_ref[j, pl.ds(rows[j], n), :].astype(BF16)
        ref = sent_ref if j < half else kept_ref
        ref[j % half // GROUP, j % GROUP] = window
    lane = lax.broadcasted_iota(jnp.int32, (1, LANES), 1)
    ids = jnp.zeros((1, LANES), jnp.int32)
    for r in range(live_ref.shape[1]):
        for k in range(slots):
            node = jnp.where(k < live_ref[0, r], ids_ref[0, r, k], -1)
            ids = jnp.where(lane == r * slots + k, node, ids)
    line_ref[...] = ids.astype(F32)


def row_place(column, base):
    count = column.shape[0]
    lane = lax.broadcasted_iota(jnp.int32, (count, LANES), 1)
    sub = lax.broadcasted_iota(jnp.int32, (count, LANES), 0)
    return jnp.sum(jnp.where(lane == sub + base, column, 0.0), axis=0, keepdims=True)


def spectra(windows, col, row):
    n = PATCH
    x = jnp.concatenate(windows, axis=0)
    hi, lo = split(dot(jnp.concatenate([x, x], axis=1), col))

    def stack(v):
        return jnp.concatenate(
            [
                jnp.concatenate([v[:n, :n], v[n:, :n]], axis=1),
                jnp.concatenate([v[:n, n:], v[n:, n:]], axis=1),
            ],
            axis=0,
        )

    hi, lo = stack(hi), stack(lo)
    f = dot(row, jnp.concatenate([hi, hi, lo], axis=0))
    return [(f[:n, :n], f[n:, :n]), (f[:n, n:], f[n:, n:])]


def correlate(first, second, inv_row, inv_col):
    n = PATCH
    count = len(first)
    lane = lax.broadcasted_iota(jnp.int32, (n, n), 1)
    low = lane <= n // 2
    crosses = []
    mag_sums = []
    for (r1, i1), (r2, i2) in zip(first, second):
        cross_r = r1 * r2 + i1 * i2
        cross_i = r1 * i2 - i1 * r2
        mag = jnp.sqrt(cross_r * cross_r + cross_i * cross_i)
        crosses.append((cross_r, cross_i, mag))
        mag_sums.append(jnp.sum(mag, axis=0, keepdims=True))
    mean = jnp.sum(jnp.concatenate(mag_sums, axis=0), axis=1, keepdims=True) / float(n * n)
    extra = 0.1 * mean + 1e-06
    surfaces = []
    sums = []
    for p in range(count):
        cross_r, cross_i, mag = crosses[p]
        inverse = 1.0 / (mag + extra[p : p + 1])
        g_r = cross_r * inverse
        g_i = cross_i * inverse
        g = jnp.concatenate([jnp.where(low, g_r, g_i), jnp.where(low, -g_i, g_r)], axis=0)
        hi, lo = split(g)
        b = dot(inv_row, jnp.concatenate([hi, hi, lo], axis=0))
        bhi, blo = split(b)
        surface = dot(jnp.concatenate([bhi, bhi, blo], axis=1), inv_col)
        surfaces.append(surface)
        sums.append(jnp.sum(surface, axis=0, keepdims=True))
    centre = jnp.sum(jnp.concatenate(sums, axis=0), axis=1, keepdims=True) / float(n * n)
    squares = []
    tops = []
    for p in range(count):
        deviation = surfaces[p] - centre[p : p + 1]
        squares.append(jnp.sum(deviation * deviation, axis=0, keepdims=True))
        tops.append(jnp.max(surfaces[p], axis=0, keepdims=True))
    variance = jnp.sum(jnp.concatenate(squares, axis=0), axis=1, keepdims=True) / float(n * n)
    top = jnp.max(jnp.concatenate(tops, axis=0), axis=1, keepdims=True)
    scale = 2.0 / jnp.sqrt(variance + 1e-06)
    sub = lax.broadcasted_iota(jnp.int32, (n, n), 0)
    sub_coord = ((sub + n // 2) % n - n // 2).astype(F32)
    columns = []
    rows = []
    edges = []
    for p in range(count):
        e = jnp.exp((surfaces[p] - top[p : p + 1]) * scale[p : p + 1])
        columns.append(jnp.sum(e, axis=0, keepdims=True))
        rows.append(jnp.sum(e * sub_coord, axis=0, keepdims=True))
        edges.append(e[n // 2 : n // 2 + 1, :])
    columns = jnp.concatenate(columns, axis=0)
    rows = jnp.concatenate(rows, axis=0)
    edges = jnp.concatenate(edges, axis=0)
    lane = lax.broadcasted_iota(jnp.int32, (count, n), 1)
    lane_coord = ((lane + n // 2) % n - n // 2).astype(F32)

    def total(v):
        return jnp.sum(v, axis=1, keepdims=True)

    unit = float(n // 8)
    norm = 1.0 / total(columns)
    row_shift = total(rows) * norm / unit
    col_shift = total(columns * lane_coord) * norm / unit
    row_edge = total(edges) * norm * (float(n) / unit)
    col_edge = total(jnp.where(lane == n // 2, columns, 0.0)) * norm * (float(n) / unit)
    return row_shift, col_shift, -row_shift - row_edge, -col_shift - col_edge


MESH = pl.DeviceIdType.MESH


def stitch(
    half,
    rounds,
    kept_ref,
    sent,
    line,
    col_ref,
    row_ref,
    inv_row_ref,
    inv_col_ref,
    out_ref,
    kept,
    firsts,
    arrived,
    lines,
    tile_out,
    tiles,
    kept_sem,
    window_send,
    window_recv,
    line_send,
    line_recv,
    tile_send,
    tile_recv,
):
    n = PATCH
    slots = 2 * half
    parts = half // GROUP
    groups = lax.axis_size("grp")
    tile_count = lax.axis_size("tiles")
    devices = tile_count * groups
    tile_index = lax.axis_index("tiles")
    me = tile_index * groups + lax.axis_index("grp")
    strides = [1] + [tile_count // 2] * (rounds - 1)
    sides = [(tile_index // s) % 2 for s in strides]
    partners = [tile_index + s * (1 - 2 * side) for s, side in zip(strides, sides)]

    load = pltpu.make_async_copy(kept_ref, kept, kept_sem)
    load.start()
    barrier = pltpu.get_barrier_semaphore()

    def device(d):
        return (d // groups, d % groups)

    def greet(i, carry):
        pl.semaphore_signal(
            barrier, inc=1, device_id=device((me + i) % devices), device_id_type=MESH
        )
        return carry

    lax.fori_loop(1, devices, greet, 0)

    load.wait()

    def prepare(g, carry):
        for p in range(0, GROUP, 2):
            pair = spectra([kept[g, p], kept[g, p + 1]], col_ref[...], row_ref[...])
            for q in range(2):
                for c in range(2):
                    firsts[g, p + q, c] = pair[q][c]
        return carry

    lax.fori_loop(0, parts, prepare, 0)
    pl.semaphore_wait(barrier, devices - 1)

    def window_copy(r, part):
        g = r * parts + part
        return pltpu.make_async_remote_copy(
            src_ref=sent.at[g],
            dst_ref=arrived.at[g],
            send_sem=window_send.at[g],
            recv_sem=window_recv.at[g],
            device_id=(partners[r], lax.axis_index("grp")),
            device_id_type=MESH,
        )

    def line_copy(r):
        return pltpu.make_async_remote_copy(
            src_ref=line,
            dst_ref=lines.at[r],
            send_sem=line_send.at[r],
            recv_sem=line_recv.at[r],
            device_id=(partners[r], lax.axis_index("grp")),
            device_id_type=MESH,
        )

    for part in range(parts):
        for r in range(rounds):
            window_copy(r, part).start()
    for r in range(rounds):
        line_copy(r).start()

    lax.fori_loop(parts, rounds * parts, prepare, 0)

    def work(g, carry):
        r = g // parts
        pltpu.make_async_remote_copy(
            src_ref=sent.at[g],
            dst_ref=arrived.at[g],
            send_sem=window_send.at[g],
            recv_sem=window_recv.at[g],
            device_id=(partners[0], lax.axis_index("grp")),
            device_id_type=MESH,
        ).wait_recv()
        side = sides[0]
        for i in range(1, rounds):
            side = jnp.where(r == i, sides[i], side)
        seconds = []
        for p in range(0, GROUP, 2):
            seconds += spectra([arrived[g, p], arrived[g, p + 1]], col_ref[...], row_ref[...])
        a, b, c, d = correlate(
            [(firsts[g, p, 0], firsts[g, p, 1]) for p in range(GROUP)],
            seconds,
            inv_row_ref[...],
            inv_col_ref[...],
        )
        base = r * slots + (g % parts) * GROUP
        own = base + side * half
        other = base + (1 - side) * half
        row_line, col_line = carry
        return (
            row_line + row_place(a, own) + row_place(c, other),
            col_line + row_place(b, own) + row_place(d, other),
        )

    zero = jnp.zeros((1, LANES), F32)
    row_line, col_line = lax.fori_loop(0, rounds * parts, work, (zero, zero))

    lane = lax.broadcasted_iota(jnp.int32, (1, LANES), 1)
    ids = line[...]
    id_line = zero
    for r in range(rounds):
        line_copy(r).wait()
        theirs = pltpu.roll(lines[r], jnp.where(sides[r] == 0, half, LANES - half), 1)
        in_round = (lane >= r * slots) & (lane < (r + 1) * slots)
        mine = (lane // half) % 2 == sides[r]
        id_line = id_line + jnp.where(in_round, jnp.where(mine, ids, theirs), 0.0)
    tile = jnp.concatenate([row_line, col_line, id_line, zero], axis=0)
    tile = pltpu.roll(tile, (me % PACK) * (LANES // PACK), 1)
    tile_out[...] = tile
    tiles[me] = tile

    def tile_copy(i, slot):
        return pltpu.make_async_remote_copy(
            src_ref=tile_out,
            dst_ref=tiles.at[slot],
            send_sem=tile_send.at[i],
            recv_sem=tile_recv.at[slot],
            device_id=device((me + i) % devices),
            device_id_type=MESH,
        )

    def start(i, carry):
        tile_copy(i, me).start()
        return carry

    def receive(i, carry):
        tile_copy(i, (me + i) % devices).wait_recv()
        return carry

    def drain(i, carry):
        tile_copy(i, me).wait_send()
        return carry

    lax.fori_loop(1, devices, start, 0)
    for part in range(parts):
        for r in range(rounds):
            window_copy(r, part).wait_send()
    lax.fori_loop(1, devices, receive, 0)

    node = lax.broadcasted_iota(jnp.int32, (NODE_DEV, LANES), 0).astype(F32)
    first_node = (me * NODE_DEV).astype(F32)
    onehots = []
    values = []
    for g in range(devices // PACK):
        tile = tiles[g * PACK]
        for i in range(1, PACK):
            tile = tile + tiles[g * PACK + i]
        onehots.append(jnp.where(tile[2:3] - first_node == node, 1.0, 0.0).astype(BF16))
        hi = tile.astype(BF16).astype(F32)
        rest = tile - hi
        mid = rest.astype(BF16).astype(F32)
        values.append(jnp.concatenate([hi, mid, rest - mid, jnp.zeros_like(hi)], axis=0).astype(BF16))
    result = lax.dot_general(
        jnp.concatenate(values, axis=1),
        jnp.concatenate(onehots, axis=1),
        (((1,), (1,)), ((), ())),
        preferred_element_type=F32,
    )
    out_ref[0:2] = result[0:2]
    out_ref[2:4] = result[4:6] + result[8:10]
    lax.fori_loop(1, devices, drain, 0)


def on_device(strips, edge_colour, patch_offsets, patch_live, node_ids):
    rounds, height, width = strips.shape
    n = PATCH
    slot_count = patch_offsets.shape[2]
    half = slot_count // 2
    parts = half // GROUP
    groups = rounds * parts
    devices = lax.axis_size("tiles") * lax.axis_size("grp")
    whole = pl.BlockSpec(memory_space=VMEM)
    anywhere = pl.BlockSpec(memory_space=pl.ANY)
    sem = pltpu.SemaphoreType.DMA
    windows = (groups, GROUP, n, n)
    window_spec = pl.BlockSpec((parts, GROUP, n, n), lambda r, *_: (r, 0, 0, 0))
    kept, sent, line = pl.pallas_call(
        functools.partial(extract, half),
        out_shape=[jax.ShapeDtypeStruct(windows, BF16)] * 2 + [jax.ShapeDtypeStruct((1, LANES), F32)],
        grid_spec=pltpu.PrefetchScalarGridSpec(
            num_scalar_prefetch=4,
            grid=(rounds,),
            in_specs=[pl.BlockSpec((1, height, width), lambda r, colour, *_: (colour[0, r], 0, 0))],
            out_specs=[window_spec, window_spec, pl.BlockSpec((1, LANES), lambda r, *_: (0, 0))],
            scratch_shapes=[pltpu.VMEM((slot_count, n + 16, n), F32)],
        ),
        name="extract",
    )(edge_colour, jnp.transpose(patch_offsets, (0, 1, 3, 2)), patch_live, node_ids, strips)
    sums = pl.pallas_call(
        functools.partial(stitch, half, rounds),
        out_shape=jax.ShapeDtypeStruct((4, NODE_DEV), F32),
        in_specs=[anywhere] * 2 + [whole] * 5,
        out_specs=whole,
        scratch_shapes=[
            pltpu.VMEM(windows, BF16),
            pltpu.VMEM((groups, GROUP, 2, n, n), F32),
            pltpu.VMEM(windows, BF16),
            pltpu.VMEM((rounds, 1, LANES), F32),
            pltpu.VMEM((4, LANES), F32),
            pltpu.VMEM((devices, 4, LANES), F32),
            sem(()),
            sem((groups,)),
            sem((groups,)),
            sem((rounds,)),
            sem((rounds,)),
            sem((devices,)),
            sem((devices,)),
        ],
        compiler_params=pltpu.CompilerParams(collective_id=0, has_side_effects=True),
        name="stitch",
    )(kept, sent, line, *(jnp.asarray(t) for t in tables()))
    return sums[0:2] + sums[2:4]


def solution(mesh):
    placed = (
        P(("tiles", "grp"), None, None),
        P(("tiles", "grp"), None),
        P(("tiles", "grp"), None, None, None),
        P(("tiles", "grp"), None),
        P(("tiles", "grp"), None, None),
    )
    return jax.shard_map(
        on_device, mesh=mesh, in_specs=placed, out_specs=P(None, ("tiles", "grp")), check_vma=False
    )
```

time: 49.6 us -> 34.9 us (0.70)
  waiting for transfers between devices: 7.9 us -> 0 us
  local copies, waits for them, and re-layouts: 7.5 us -> 0 us
  starting transfers between devices: 6.24 us -> 0 us
  Pallas kernels: 27.4 us -> 33.3 us
  other arithmetic: 0.22 us -> 1.32 us
    ppermute x4 -> x0, waiting for transfers between devices: 7.9 us -> none  [the longest x2 7.9 us: on_device(): lines += [mine, lax.ppermute(other, 'tiles', pairs)]]
    pallas_call x3 -> x1, Pallas kernels: 22.8 us -> 29.1 us  [on_device(): pl.pallas_call(functools.partial(stitch, half, rounds), out_shape=jax.Sha...]
    ppermute x4 -> x0, starting transfers between devices: 6.24 us -> none  [the longest x2 4.41 us: on_device(): seconds.append(lax.ppermute(sent[r:r + 1], 'tiles', pairs))]
    unnamed x10 -> x0, local copies, waits for them, and re-layouts: 4.04 us -> none
    slice x2 -> x0, local copies, waits for them, and re-layouts: 2.94 us -> none  [the longest x1 1.87 us: on_device(): args = [kept[r:r + 1], seconds[r], col, row, inv_row, inv_col]]
    add x0 -> x1, other arithmetic: none -> 1.32 us  [on_device(): return sums[0:2] + sums[2:4]]
    broadcast_in_dim x1 -> x0, local copies, waits for them, and re-layouts: 0.52 us -> none  [on_device(): jnp.concatenate([id_line, jnp.full((LANES - id_line.shape[0],), 0.0, F32)])]
  transfers between devices with their start and end apart: 4 -> 0, of which waited for: 1 -> 0; matrix products, arithmetic and copies ran while one was open for 5% -> 0% of each run, Pallas kernels for 12% -> 0%
where the time goes in v2:
time: 34.9 us; the launch traced here: 34.7 us
  Pallas kernels  33.3 us (95%)
  other arithmetic  1.32 us (4%)
    pallas_call x1, Pallas kernels, on_device(): pl.pallas_call(functools.partial(stitch, half, rounds), out_shape=jax.Sha...  29.1 us
    pallas_call x1, Pallas kernels, on_device(): pl.pallas_call(functools.partial(extract, half), out_shape=[jax.ShapeDtyp...  4.2 us
    add x1, other arithmetic, on_device(): return sums[0:2] + sums[2:4]  1.32 us

profile of v2, /device:TPU:0, one launch (start us, length us, event | category | flops | bytes accessed | tf_op | source)
XLA Modules:
  0.0 34.7 jit_solution(10539404458828209250)
XLA Ops:
  0.0 4.2 %extract.1 = (bf16[4,4,128,128]{3,2,1,0:T(8,128)(2,1)}, bf16[4,4,128,128]{3,2,1,0:T(8,128)(2,1)}, f32[1,128]{1,0:T(1,128)}) custom-call(s32[1,2]{1,0:T(1,128)} %colour_ref.1, s32[1,2,2,16]{3,2,1,0:T(2,128)} %bitcast.1, s32[1,2]{1,0:T(1,128)} %live_ref.1, s32[1,2,16]{2,1,0:T(2,128)} %ids_ref.1, bf16[2,256,4096]{2,1,0:T(8,128)(2,1)} %strip_ref.1), custom_call_target="tpu_custom_call" | custom-call | tf_op jit(solution)/shard_map/extract/pallas_call | solution.py:392
  4.2 29.1 %stitch.1 = f32[4,128]{1,0:T(4,128)} custom-call(bf16[4,4,128,128]{3,2,1,0:T(8,128)(2,1)} %get-tuple-element.8.kept_ref, bf16[4,4,128,128]{3,2,1,0:T(8,128)(2,1)} %get-tuple-element.9.sent, f32[1,128]{1,0:T(1,128)} %get-tuple-element.10.line, bf16[256,256]{1,0:T(8,128)(2,1)} %constant.8.clone.col_ref, bf16[256,768]{1,0:T(8,128)(2,1)} %constant.9.clone.row_ref, ...), custom_call_target="tpu_custom_call" | custom-call | tf_op jit(solution)/shard_map/stitch/pallas_call | solution.py:404
  33.4 1.3 %slice_add_fusion = f32[2,128]{1,0:T(2,128)} fusion(f32[4,128]{1,0:T(4,128)} %stitch.1), kind=kLoop, calls=%fused_computation | loop fusion | flops 256 | bytes 3072 | tf_op jit(solution)/shard_map/add | solution.py:427

commit v3 on v2

--- a/solution.py
+++ b/solution.py
@@ -206,6 +206,7 @@
     line_recv,
     tile_send,
     tile_recv,
+    hello,
 ):
     n = PATCH
     slots = 2 * half
@@ -226,13 +227,32 @@
     def device(d):
         return (d // groups, d % groups)
 
-    def greet(i, carry):
+    neighbours = []
+    stride = 1
+    while stride < tile_count:
+        bit = (tile_index // stride) % 2
+        neighbours.append((tile_index + stride * (1 - 2 * bit), lax.axis_index("grp")))
+        stride *= 2
+    stride = 1
+    while stride < groups:
+        bit = (lax.axis_index("grp") // stride) % 2
+        neighbours.append((tile_index, lax.axis_index("grp") + stride * (1 - 2 * bit)))
+        stride *= 2
+    stages = len(neighbours)
+    for at in neighbours:
+        pl.semaphore_signal(barrier, inc=1, device_id=at, device_id_type=MESH)
+
+    def neighbour(stage):
+        tile, group = neighbours[0]
+        for i in range(1, stages):
+            tile = jnp.where(stage == i, neighbours[i][0], tile)
+            group = jnp.where(stage == i, neighbours[i][1], group)
+        return tile, group
+
+    def hail(stage):
         pl.semaphore_signal(
-            barrier, inc=1, device_id=device((me + i) % devices), device_id_type=MESH
-        )
-        return carry
-
-    lax.fori_loop(1, devices, greet, 0)
+            hello.at[stage], inc=1, device_id=neighbour(stage), device_id_type=MESH
+        )
 
     load.wait()
 
@@ -244,8 +264,8 @@
                     firsts[g, p + q, c] = pair[q][c]
         return carry
 
-    lax.fori_loop(0, parts, prepare, 0)
-    pl.semaphore_wait(barrier, devices - 1)
+    lax.fori_loop(0, 1, prepare, 0)
+    pl.semaphore_wait(barrier, stages)
 
     def window_copy(r, part):
         g = r * parts + part
@@ -274,10 +294,16 @@
     for r in range(rounds):
         line_copy(r).start()
 
-    lax.fori_loop(parts, rounds * parts, prepare, 0)
+    early = stages - rounds * parts
+    for i in range(early):
+        hail(i)
+        if i == early - 1:
+            lax.fori_loop(1, rounds * parts, prepare, 0)
+        pl.semaphore_wait(hello.at[i], 1)
 
     def work(g, carry):
         r = g // parts
+        hail(early + g)
         pltpu.make_async_remote_copy(
             src_ref=sent.at[g],
             dst_ref=arrived.at[g],
@@ -302,6 +328,7 @@
         own = base + side * half
         other = base + (1 - side) * half
         row_line, col_line = carry
+        pl.semaphore_wait(hello.at[early + g], 1)
         return (
             row_line + row_place(a, own) + row_place(c, other),
             col_line + row_place(b, own) + row_place(d, other),
@@ -420,6 +447,7 @@
             sem((rounds,)),
             sem((devices,)),
             sem((devices,)),
+            pltpu.SemaphoreType.REGULAR((devices.bit_length() - 1,)),
         ],
         compiler_params=pltpu.CompilerParams(collective_id=0, has_side_effects=True),
         name="stitch",

time: 34.9 us -> 34.2 us (0.980)
  Pallas kernels: 33.3 us -> 32.6 us
    pallas_call x1, Pallas kernels: 29.1 us -> 28.4 us  [on_device(): pl.pallas_call(functools.partial(stitch, half, rounds), out_shape=jax.Sha...]
where the time goes in v3:
time: 34.2 us; the launch traced here: 34 us
  Pallas kernels  32.6 us (95%)
  other arithmetic  1.32 us (4%)
    pallas_call x1, Pallas kernels, on_device(): pl.pallas_call(functools.partial(stitch, half, rounds), out_shape=jax.Sha...  28.4 us
    pallas_call x1, Pallas kernels, on_device(): pl.pallas_call(functools.partial(extract, half), out_shape=[jax.ShapeDtyp...  4.2 us
    add x1, other arithmetic, on_device(): return sums[0:2] + sums[2:4]  1.32 us

profile of v3, /device:TPU:0, one launch (start us, length us, event | category | flops | bytes accessed | tf_op | source)
XLA Modules:
  0.0 34.0 jit_solution(13488542828131645466)
XLA Ops:
  0.0 4.2 %extract.1 = (bf16[4,4,128,128]{3,2,1,0:T(8,128)(2,1)}, bf16[4,4,128,128]{3,2,1,0:T(8,128)(2,1)}, f32[1,128]{1,0:T(1,128)}) custom-call(s32[1,2]{1,0:T(1,128)} %colour_ref.1, s32[1,2,2,16]{3,2,1,0:T(2,128)} %bitcast.1, s32[1,2]{1,0:T(1,128)} %live_ref.1, s32[1,2,16]{2,1,0:T(2,128)} %ids_ref.1, bf16[2,256,4096]{2,1,0:T(8,128)(2,1)} %strip_ref.1), custom_call_target="tpu_custom_call" | custom-call | tf_op jit(solution)/shard_map/extract/pallas_call | solution.py:419
  4.2 28.4 %stitch.1 = f32[4,128]{1,0:T(4,128)} custom-call(bf16[4,4,128,128]{3,2,1,0:T(8,128)(2,1)} %get-tuple-element.8.kept_ref, bf16[4,4,128,128]{3,2,1,0:T(8,128)(2,1)} %get-tuple-element.9.sent, f32[1,128]{1,0:T(1,128)} %get-tuple-element.10.line, bf16[256,256]{1,0:T(8,128)(2,1)} %constant.8.clone.col_ref, bf16[256,768]{1,0:T(8,128)(2,1)} %constant.9.clone.row_ref, ...), custom_call_target="tpu_custom_call" | custom-call | tf_op jit(solution)/shard_map/stitch/pallas_call | solution.py:431
  32.7 1.3 %slice_add_fusion = f32[2,128]{1,0:T(2,128)} fusion(f32[4,128]{1,0:T(4,128)} %stitch.1), kind=kLoop, calls=%fused_computation | loop fusion | flops 256 | bytes 3072 | tf_op jit(solution)/shard_map/add | solution.py:455

commit v4 on v3

--- a/solution.py
+++ b/solution.py
@@ -128,17 +128,25 @@
     mean = jnp.sum(jnp.concatenate(mag_sums, axis=0), axis=1, keepdims=True) / float(n * n)
     extra = 0.1 * mean + 1e-06
     surfaces = []
+    packed = []
     sums = []
     for p in range(count):
         cross_r, cross_i, mag = crosses[p]
         inverse = 1.0 / (mag + extra[p : p + 1])
         g_r = cross_r * inverse
         g_i = cross_i * inverse
-        g = jnp.concatenate([jnp.where(low, g_r, g_i), jnp.where(low, -g_i, g_r)], axis=0)
-        hi, lo = split(g)
+        packed.append(
+            split(jnp.concatenate([jnp.where(low, g_r, g_i), jnp.where(low, -g_i, g_r)], axis=0))
+        )
+    surfaces_wide = []
+    for p in range(0, count, 2):
+        hi = jnp.concatenate([packed[p][0], packed[p + 1][0]], axis=1)
+        lo = jnp.concatenate([packed[p][1], packed[p + 1][1]], axis=1)
         b = dot(inv_row, jnp.concatenate([hi, hi, lo], axis=0))
-        bhi, blo = split(b)
-        surface = dot(jnp.concatenate([bhi, bhi, blo], axis=1), inv_col)
+        bhi, blo = split(jnp.concatenate([b[:, :n], b[:, n:]], axis=0))
+        wide = dot(jnp.concatenate([bhi, bhi, blo], axis=1), inv_col)
+        surfaces_wide += [wide[:n], wide[n:]]
+    for surface in surfaces_wide:
         surfaces.append(surface)
         sums.append(jnp.sum(surface, axis=0, keepdims=True))
     centre = jnp.sum(jnp.concatenate(sums, axis=0), axis=1, keepdims=True) / float(n * n)

time: 34.2 us -> 34 us (level)
  no operation moved by 1% of the time
where the time goes in v4:
time: 34 us; the launch traced here: 33.7 us
  Pallas kernels  32.4 us (95%)
  other arithmetic  1.32 us (4%)
    pallas_call x1, Pallas kernels, on_device(): pl.pallas_call(functools.partial(stitch, half, rounds), out_shape=jax.Sha...  28.2 us
    pallas_call x1, Pallas kernels, on_device(): pl.pallas_call(functools.partial(extract, half), out_shape=[jax.ShapeDtyp...  4.2 us
    add x1, other arithmetic, on_device(): return sums[0:2] + sums[2:4]  1.32 us

profile of v4, /device:TPU:0, one launch (start us, length us, event | category | flops | bytes accessed | tf_op | source)
XLA Modules:
  0.0 33.7 jit_solution(16859704907427774619)
XLA Ops:
  0.0 4.2 %extract.1 = (bf16[4,4,128,128]{3,2,1,0:T(8,128)(2,1)}, bf16[4,4,128,128]{3,2,1,0:T(8,128)(2,1)}, f32[1,128]{1,0:T(1,128)}) custom-call(s32[1,2]{1,0:T(1,128)} %colour_ref.1, s32[1,2,2,16]{3,2,1,0:T(2,128)} %bitcast.1, s32[1,2]{1,0:T(1,128)} %live_ref.1, s32[1,2,16]{2,1,0:T(2,128)} %ids_ref.1, bf16[2,256,4096]{2,1,0:T(8,128)(2,1)} %strip_ref.1), custom_call_target="tpu_custom_call" | custom-call | tf_op jit(solution)/shard_map/extract/pallas_call | solution.py:427
  4.2 28.2 %stitch.1 = f32[4,128]{1,0:T(4,128)} custom-call(bf16[4,4,128,128]{3,2,1,0:T(8,128)(2,1)} %get-tuple-element.8.kept_ref, bf16[4,4,128,128]{3,2,1,0:T(8,128)(2,1)} %get-tuple-element.9.sent, f32[1,128]{1,0:T(1,128)} %get-tuple-element.10.line, bf16[256,256]{1,0:T(8,128)(2,1)} %constant.8.clone.col_ref, bf16[256,768]{1,0:T(8,128)(2,1)} %constant.9.clone.row_ref, ...), custom_call_target="tpu_custom_call" | custom-call | tf_op jit(solution)/shard_map/stitch/pallas_call | solution.py:439
  32.4 1.3 %slice_add_fusion = f32[2,128]{1,0:T(2,128)} fusion(f32[4,128]{1,0:T(4,128)} %stitch.1), kind=kLoop, calls=%fused_computation | loop fusion | flops 256 | bytes 3072 | tf_op jit(solution)/shard_map/add | solution.py:463

commit v5 on v4

--- a/solution.py
+++ b/solution.py
@@ -54,29 +54,44 @@
     return jnp.dot(a, b, preferred_element_type=F32)
 
 
-def extract(half, colour_ref, offset_ref, live_ref, ids_ref, strip_ref, kept_ref, sent_ref, line_ref, tmp_ref):
+def extract(half, colour_ref, offset_ref, live_ref, ids_ref, strips_ref, kept_ref, sent_ref, line_ref, blocks, tmp_ref, sems):
     n = PATCH
     slots = 2 * half
-    rnd = pl.program_id(0)
+    rounds, height, width = strips_ref.shape
+    parts = half // GROUP
     tile = lax.axis_index("tiles")
-    side = jnp.where(rnd == 0, tile % 2, (tile // (lax.axis_size("tiles") // 2)) % 2)
-    height, width = strip_ref.shape[1], strip_ref.shape[2]
-    rows = []
-    for j in range(slots):
-        k = (side * half + half + j) % slots
-        row, column = offset_ref[0, rnd, 0, k], offset_ref[0, rnd, 1, k]
-        left = jnp.minimum(lax.div(column, LANES), width // LANES - 2) * LANES
-        upper = jnp.minimum(lax.div(row, 16), (height - n) // 16 - 1) * 16
-        block = strip_ref[
-            0, pl.ds(pl.multiple_of(upper, 16), n + 16), pl.ds(pl.multiple_of(left, LANES), 2 * LANES)
-        ].astype(F32)
-        shift = lax.rem(2 * LANES - (column - left), 2 * LANES)
-        tmp_ref[j] = pltpu.roll(block, shift, 1)[:, :n]
-        rows.append(row - upper)
-    for j in range(slots):
-        window = tmp_ref[j, pl.ds(rows[j], n), :].astype(BF16)
-        ref = sent_ref if j < half else kept_ref
-        ref[j % half // GROUP, j % GROUP] = window
+    last = lax.axis_size("tiles") // 2
+    places = []
+    for which in (1, 0):
+        for r in range(rounds):
+            side = (tile // (1 if r == 0 else last)) % 2
+            for j in range(half):
+                k = ((side + which) % 2) * half + j
+                row, column = offset_ref[0, r, 0, k], offset_ref[0, r, 1, k]
+                left = jnp.minimum(lax.div(column, LANES), width // LANES - 2) * LANES
+                upper = jnp.minimum(lax.div(row, 16), (height - n) // 16 - 1) * 16
+                i = len(places)
+                copy = pltpu.make_async_copy(
+                    strips_ref.at[
+                        colour_ref[0, r],
+                        pl.ds(pl.multiple_of(upper, 16), n + 16),
+                        pl.ds(pl.multiple_of(left, LANES), 2 * LANES),
+                    ],
+                    blocks.at[i],
+                    sems.at[i],
+                )
+                copy.start()
+                shift = lax.rem(2 * LANES - (column - left), 2 * LANES)
+                ref = sent_ref if which else kept_ref
+                places.append((copy, shift, row - upper, ref, r * parts + j // GROUP, j % GROUP))
+    for start in range(0, len(places), GROUP):
+        for i in range(start, start + GROUP):
+            copy, shift = places[i][:2]
+            copy.wait()
+            tmp_ref[i] = pltpu.roll(blocks[i].astype(F32), shift, 1)[:, :n]
+        for i in range(start, start + GROUP):
+            _, _, ahead, ref, g, p = places[i]
+            ref[g, p] = tmp_ref[i, pl.ds(ahead, n), :].astype(BF16)
     lane = lax.broadcasted_iota(jnp.int32, (1, LANES), 1)
     ids = jnp.zeros((1, LANES), jnp.int32)
     for r in range(live_ref.shape[1]):
@@ -427,13 +442,13 @@
     kept, sent, line = pl.pallas_call(
         functools.partial(extract, half),
         out_shape=[jax.ShapeDtypeStruct(windows, BF16)] * 2 + [jax.ShapeDtypeStruct((1, LANES), F32)],
-        grid_spec=pltpu.PrefetchScalarGridSpec(
-            num_scalar_prefetch=4,
-            grid=(rounds,),
-            in_specs=[pl.BlockSpec((1, height, width), lambda r, colour, *_: (colour[0, r], 0, 0))],
-            out_specs=[window_spec, window_spec, pl.BlockSpec((1, LANES), lambda r, *_: (0, 0))],
-            scratch_shapes=[pltpu.VMEM((slot_count, n + 16, n), F32)],
-        ),
+        in_specs=[pl.BlockSpec(memory_space=SMEM)] * 4 + [anywhere],
+        out_specs=[whole] * 3,
+        scratch_shapes=[
+            pltpu.VMEM((rounds * slot_count, n + 16, 2 * LANES), BF16),
+            pltpu.VMEM((rounds * slot_count, n + 16, n), F32),
+            sem((rounds * slot_count,)),
+        ],
         name="extract",
     )(edge_colour, jnp.transpose(patch_offsets, (0, 1, 3, 2)), patch_live, node_ids, strips)
     sums = pl.pallas_call(

time: 34 us -> 35.7 us (1.050)
  Pallas kernels: 32.4 us -> 34.1 us
    pallas_call x1, Pallas kernels: 4.2 us -> 5.93 us  [on_device(): pl.pallas_call(functools.partial(extract, half), out_shape=[jax.ShapeDtyp...]
where the time goes in v5:
time: 35.7 us; the launch traced here: 35.5 us
  Pallas kernels  34.1 us (96%)
  other arithmetic  1.32 us (4%)
    pallas_call x1, Pallas kernels, on_device(): pl.pallas_call(functools.partial(stitch, half, rounds), out_shape=jax.Sha...  28.2 us
    pallas_call x1, Pallas kernels, on_device(): pl.pallas_call(functools.partial(extract, half), out_shape=[jax.ShapeDtyp...  5.93 us
    add x1, other arithmetic, on_device(): return sums[0:2] + sums[2:4]  1.32 us

profile of v5, /device:TPU:0, one launch (start us, length us, event | category | flops | bytes accessed | tf_op | source)
XLA Modules:
  0.0 35.5 jit_solution(8314145123319644421)
XLA Ops:
  0.0 5.9 %extract.1 = (bf16[4,4,128,128]{3,2,1,0:T(8,128)(2,1)}, bf16[4,4,128,128]{3,2,1,0:T(8,128)(2,1)}, f32[1,128]{1,0:T(1,128)}) custom-call(s32[1,2]{1,0:T(1,128)} %colour_ref.1, s32[1,2,2,16]{3,2,1,0:T(2,128)} %bitcast.1, s32[1,2]{1,0:T(1,128)} %live_ref.1, s32[1,2,16]{2,1,0:T(2,128)} %ids_ref.1, bf16[2,256,4096]{2,1,0:T(8,128)(2,1)} %strips_ref.1), custom_call_target="tpu_custom_call" | custom-call | tf_op jit(solution)/shard_map/extract/pallas_call | solution.py:442
  5.9 28.2 %stitch.1 = f32[4,128]{1,0:T(4,128)} custom-call(bf16[4,4,128,128]{3,2,1,0:T(8,128)(2,1)} %get-tuple-element.8.kept_ref, bf16[4,4,128,128]{3,2,1,0:T(8,128)(2,1)} %get-tuple-element.9.sent, f32[1,128]{1,0:T(1,128)} %get-tuple-element.10.line, bf16[256,256]{1,0:T(8,128)(2,1)} %constant.8.clone.col_ref, bf16[256,768]{1,0:T(8,128)(2,1)} %constant.9.clone.row_ref, ...), custom_call_target="tpu_custom_call" | custom-call | tf_op jit(solution)/shard_map/stitch/pallas_call | solution.py:454
  34.1 1.3 %slice_add_fusion = f32[2,128]{1,0:T(2,128)} fusion(f32[4,128]{1,0:T(4,128)} %stitch.1), kind=kLoop, calls=%fused_computation | loop fusion | flops 256 | bytes 3072 | tf_op jit(solution)/shard_map/add | solution.py:478

commit v6 on v4

--- a/solution.py
+++ b/solution.py
@@ -297,7 +297,7 @@
         )
 
     for part in range(parts):
-        for r in range(rounds):
+        for r in reversed(range(rounds)):
             window_copy(r, part).start()
     for r in range(rounds):
         line_copy(r).start()

time: 34 us -> 34 us (level)
  no operation moved by 1% of the time
where the time goes in v6:
time: 34 us; the launch traced here: 33.7 us
  Pallas kernels  32.4 us (95%)
  other arithmetic  1.32 us (4%)
    pallas_call x1, Pallas kernels, on_device(): pl.pallas_call(functools.partial(stitch, half, rounds), out_shape=jax.Sha...  28.2 us
    pallas_call x1, Pallas kernels, on_device(): pl.pallas_call(functools.partial(extract, half), out_shape=[jax.ShapeDtyp...  4.2 us
    add x1, other arithmetic, on_device(): return sums[0:2] + sums[2:4]  1.32 us

profile of v6, /device:TPU:0, one launch (start us, length us, event | category | flops | bytes accessed | tf_op | source)
XLA Modules:
  0.0 33.7 jit_solution(10226884157062922208)
XLA Ops:
  0.0 4.2 %extract.1 = (bf16[4,4,128,128]{3,2,1,0:T(8,128)(2,1)}, bf16[4,4,128,128]{3,2,1,0:T(8,128)(2,1)}, f32[1,128]{1,0:T(1,128)}) custom-call(s32[1,2]{1,0:T(1,128)} %colour_ref.1, s32[1,2,2,16]{3,2,1,0:T(2,128)} %bitcast.1, s32[1,2]{1,0:T(1,128)} %live_ref.1, s32[1,2,16]{2,1,0:T(2,128)} %ids_ref.1, bf16[2,256,4096]{2,1,0:T(8,128)(2,1)} %strip_ref.1), custom_call_target="tpu_custom_call" | custom-call | tf_op jit(solution)/shard_map/extract/pallas_call | solution.py:427
  4.2 28.2 %stitch.1 = f32[4,128]{1,0:T(4,128)} custom-call(bf16[4,4,128,128]{3,2,1,0:T(8,128)(2,1)} %get-tuple-element.8.kept_ref, bf16[4,4,128,128]{3,2,1,0:T(8,128)(2,1)} %get-tuple-element.9.sent, f32[1,128]{1,0:T(1,128)} %get-tuple-element.10.line, bf16[256,256]{1,0:T(8,128)(2,1)} %constant.8.clone.col_ref, bf16[256,768]{1,0:T(8,128)(2,1)} %constant.9.clone.row_ref, ...), custom_call_target="tpu_custom_call" | custom-call | tf_op jit(solution)/shard_map/stitch/pallas_call | solution.py:439
  32.4 1.3 %slice_add_fusion = f32[2,128]{1,0:T(2,128)} fusion(f32[4,128]{1,0:T(4,128)} %stitch.1), kind=kLoop, calls=%fused_computation | loop fusion | flops 256 | bytes 3072 | tf_op jit(solution)/shard_map/add | solution.py:463

commit v7 on v4

--- a/solution.py
+++ b/solution.py
@@ -13,7 +13,7 @@
 NODE_DEV = 128
 LANES = 128
 PACK = 4
-GROUP = 4
+GROUP = 2
 
 F32 = jnp.float32
 BF16 = jnp.bfloat16
@@ -308,10 +308,16 @@
         if i == early - 1:
             lax.fori_loop(1, rounds * parts, prepare, 0)
         pl.semaphore_wait(hello.at[i], 1)
+    if early <= 0:
+        lax.fori_loop(1, rounds * parts, prepare, 0)
 
     def work(g, carry):
         r = g // parts
-        hail(early + g)
+
+        @pl.when(g + early >= 0)
+        def _():
+            hail(early + g)
+
         pltpu.make_async_remote_copy(
             src_ref=sent.at[g],
             dst_ref=arrived.at[g],
@@ -336,7 +342,11 @@
         own = base + side * half
         other = base + (1 - side) * half
         row_line, col_line = carry
-        pl.semaphore_wait(hello.at[early + g], 1)
+
+        @pl.when(g + early >= 0)
+        def _():
+            pl.semaphore_wait(hello.at[early + g], 1)
+
         return (
             row_line + row_place(a, own) + row_place(c, other),
             col_line + row_place(b, own) + row_place(d, other),

time: 34 us -> 34.5 us (1.015)
  Pallas kernels: 32.4 us -> 33 us
    pallas_call x1, Pallas kernels: 28.2 us -> 28.8 us  [on_device(): pl.pallas_call(functools.partial(stitch, half, rounds), out_shape=jax.Sha...]
where the time goes in v7:
time: 34.5 us; the launch traced here: 34.3 us
  Pallas kernels  33 us (96%)
  other arithmetic  1.32 us (4%)
    pallas_call x1, Pallas kernels, on_device(): pl.pallas_call(functools.partial(stitch, half, rounds), out_shape=jax.Sha...  28.8 us
    pallas_call x1, Pallas kernels, on_device(): pl.pallas_call(functools.partial(extract, half), out_shape=[jax.ShapeDtyp...  4.2 us
    add x1, other arithmetic, on_device(): return sums[0:2] + sums[2:4]  1.32 us

profile of v7, /device:TPU:0, one launch (start us, length us, event | category | flops | bytes accessed | tf_op | source)
XLA Modules:
  0.0 34.3 jit_solution(8374289009066352653)
XLA Ops:
  0.0 4.2 %extract.1 = (bf16[8,2,128,128]{3,2,1,0:T(8,128)(2,1)}, bf16[8,2,128,128]{3,2,1,0:T(8,128)(2,1)}, f32[1,128]{1,0:T(1,128)}) custom-call(s32[1,2]{1,0:T(1,128)} %colour_ref.1, s32[1,2,2,16]{3,2,1,0:T(2,128)} %bitcast.1, s32[1,2]{1,0:T(1,128)} %live_ref.1, s32[1,2,16]{2,1,0:T(2,128)} %ids_ref.1, bf16[2,256,4096]{2,1,0:T(8,128)(2,1)} %strip_ref.1), custom_call_target="tpu_custom_call" | custom-call | tf_op jit(solution)/shard_map/extract/pallas_call | solution.py:437
  4.2 28.8 %stitch.1 = f32[4,128]{1,0:T(4,128)} custom-call(bf16[8,2,128,128]{3,2,1,0:T(8,128)(2,1)} %get-tuple-element.8.kept_ref, bf16[8,2,128,128]{3,2,1,0:T(8,128)(2,1)} %get-tuple-element.9.sent, f32[1,128]{1,0:T(1,128)} %get-tuple-element.10.line, bf16[256,256]{1,0:T(8,128)(2,1)} %constant.8.clone.col_ref, bf16[256,768]{1,0:T(8,128)(2,1)} %constant.9.clone.row_ref, ...), custom_call_target="tpu_custom_call" | custom-call | tf_op jit(solution)/shard_map/stitch/pallas_call | solution.py:449
  33.0 1.3 %slice_add_fusion = f32[2,128]{1,0:T(2,128)} fusion(f32[4,128]{1,0:T(4,128)} %stitch.1), kind=kLoop, calls=%fused_computation | loop fusion | flops 256 | bytes 3072 | tf_op jit(solution)/shard_map/add | solution.py:473
